TPU v7x, 32 devices: a whole 2x2x4 slice. The times are simulated.
32 devices in a mesh: grp: 2 (over y), seq: 4 (over z), outer: 4 (over x, core).
Axes of the slice: x: 2, y: 2, z: 4, core: 2. Of those that a mesh axis runs over, the one named last changes fastest.
Arguments:
- inputs: bfloat16 [32768, 512], P(('grp', 'outer', 'seq')), parts along dimension 0, may hold values from -6 to 6
- grad_out: bfloat16 [32768, 512], P(('grp', 'outer', 'seq')), parts along dimension 0, may hold values from -6 to 6
- w_query: bfloat16 [512, 512], replicated, may hold values from -0.25 to 0.25
- w_key: bfloat16 [512, 512], replicated, may hold values from -0.25 to 0.25
- w_value: bfloat16 [512, 512], replicated, may hold values from -0.25 to 0.25
- conv_taps: bfloat16 [4, 512], replicated, may hold values from -3 to 3
Outputs:
- grad_inputs: bfloat16 [32768, 512], P(('grp', 'outer', 'seq')), parts along dimension 0
- grad_wq: float32 [1024, 512], P('grp'), parts along dimension 0
- grad_wk: float32 [1024, 512], P('grp'), parts along dimension 0
- grad_wv: float32 [1024, 512], P('grp'), parts along dimension 0
- grad_conv: float32 [8, 512], P('grp'), parts along dimension 0
There are 2 independent parts, one for each index of `grp`. A program takes and returns all parts, laid end to end along the dimension named above; an argument that names none is the same for every part. Nothing has to cross between parts.
All inputs are finite; a program needn't handle non-finite values.
Results may differ from a plain program's by a relative error of at most 0.0095.
Values may be sent and summed in bfloat16 or wider, within the bound.
A program may use at most 128 MiB of HBM per device.

v0:
```python
import math

import jax
import jax.numpy as jnp
from jax import lax
from jax.sharding import PartitionSpec as P

D = 512
HEADS = 8
HEAD_DIM = 64
TAPS = 4
BLOCK = 512


def shifted(x, axis, by):
    devices = lax.axis_size(axis)
    return lax.ppermute(x, axis, [(i, (i + by) % devices) for i in range(devices)])


def from_behind(value, axis, steps):
    count = lax.axis_size(axis)
    leading, last = (max(0, -steps), min(count, count - steps))
    return lax.ppermute(value, axis, [(source, source + steps) for source in range(leading, last)])


def entering(x, axis, join, neutral, backward):
    count = lax.axis_size(axis)
    place = lax.axis_index(axis)
    ahead = count - 1 - place if backward else place
    gathered = lax.all_gather(x.astype(jnp.bfloat16), axis)
    state = jnp.zeros_like(x) + jnp.asarray(neutral, x.dtype)

    def one(step, state):
        source = count - 1 - step if backward else step
        return join(state, lax.dynamic_index_in_dim(gathered, source, 0, False).astype(x.dtype))

    return lax.fori_loop(0, ahead, one, state)


def add_states(earlier, later):
    return earlier + later


def block_grads(parts):
    queries, key_rows, value_rows, grad_rows, scales, state_prev, state_next = parts
    size = queries.shape[0]
    highest = lax.Precision.HIGHEST
    causal = lax.broadcasted_iota(jnp.int32, (size, size), 0) >= lax.broadcasted_iota(
        jnp.int32, (size, size), 1
    )
    scores = jnp.einsum("thj,shj->hts", grad_rows, value_rows, preferred_element_type=jnp.float32)
    probe = jnp.where(causal[None], scores * scales[None, :, None], 0.0).astype(jnp.bfloat16)
    grad_query = jnp.einsum("hts,shi->thi", probe, key_rows, preferred_element_type=jnp.float32)
    grad_query = grad_query + scales[:, None, None] * jnp.einsum(
        "thj,hij->thi", grad_rows.astype(jnp.float32), state_prev, precision=highest
    )
    grad_key = jnp.einsum("hts,thi->shi", probe, queries, preferred_element_type=jnp.float32)
    grad_key = grad_key + jnp.einsum(
        "shj,hij->shi", value_rows.astype(jnp.float32), state_next, precision=highest
    )
    affinity = jnp.einsum("thi,shi->hts", queries, key_rows, preferred_element_type=jnp.float32)
    mixing = jnp.where(causal[None], affinity * scales[None, :, None], 0.0).astype(jnp.bfloat16)
    grad_value = jnp.einsum("hts,thj->shj", mixing, grad_rows, preferred_element_type=jnp.float32)
    grad_value = grad_value + jnp.einsum(
        "shi,hij->shj", key_rows.astype(jnp.float32), state_next, precision=highest
    )
    return (
        grad_query.reshape(size, D).astype(jnp.bfloat16),
        grad_key.reshape(size, D).astype(jnp.bfloat16),
        grad_value.reshape(size, D).astype(jnp.bfloat16),
    )


def on_device(inputs, grad_out, w_query, w_key, w_value, conv_taps):
    length = inputs.shape[0]
    model_width = inputs.shape[1]
    highest = lax.Precision.HIGHEST
    seq_count = lax.axis_size("seq")
    seq_place = lax.axis_index("seq")
    outer_place = lax.axis_index("outer")
    offset = (outer_place * seq_count + seq_place) * length
    queries = jnp.dot(inputs, w_query, preferred_element_type=jnp.float32).astype(jnp.bfloat16)
    keys_pre = jnp.dot(inputs, w_key, preferred_element_type=jnp.float32).astype(jnp.bfloat16)
    values = jnp.dot(inputs, w_value, preferred_element_type=jnp.float32).astype(jnp.bfloat16)
    tail_rows = keys_pre[length - (TAPS - 1) :]
    wrapped = shifted(tail_rows, "seq", 1)
    across = from_behind(wrapped, "outer", 1)
    before = jnp.where(seq_place == 0, across, wrapped)
    taps = conv_taps.astype(jnp.float32)
    padded = jnp.concatenate([before, keys_pre], 0).astype(jnp.float32)
    keys = jnp.zeros((length, model_width), jnp.float32)
    for tap_index in range(TAPS):
        keys = keys + taps[tap_index] * padded[TAPS - 1 - tap_index : TAPS - 1 - tap_index + length]
    keys = keys.astype(jnp.bfloat16)
    position = (offset + jnp.arange(length, dtype=jnp.int32)).astype(jnp.float32)
    scales = 1.0 / (jnp.sqrt(position + 1.0) * math.sqrt(HEAD_DIM))
    block_count = length // BLOCK
    shape = (block_count, BLOCK, HEADS, HEAD_DIM)
    query_heads = queries.reshape(shape)
    key_heads = keys.reshape(shape)
    value_heads = values.reshape(shape)
    grad_heads = grad_out.reshape(shape)
    block_scales = scales.reshape(block_count, BLOCK)
    kv_blocks = jnp.einsum(
        "nbhi,nbhj->nhij", key_heads, value_heads, preferred_element_type=jnp.float32
    )
    scaled_queries = query_heads.astype(jnp.float32) * block_scales[:, :, None, None]
    qdo_blocks = jnp.einsum(
        "nbhi,nbhj->nhij", scaled_queries, grad_heads.astype(jnp.float32), precision=highest
    )
    kv_local = jnp.sum(kv_blocks, 0)
    qdo_local = jnp.sum(qdo_blocks, 0)
    zeros = jnp.zeros_like(kv_local)
    kv_inner = entering(kv_local, "seq", add_states, zeros, False)
    kv_group, qdo_group = lax.psum((kv_local, qdo_local), "seq")
    kv_outer = entering(kv_group, "outer", add_states, zeros, False)
    qdo_inner = entering(qdo_local, "seq", add_states, zeros, True)
    qdo_outer = entering(qdo_group, "outer", add_states, zeros, True)
    state_before = kv_outer + kv_inner
    state_after = qdo_outer + qdo_inner
    state_prev = state_before[None] + jnp.cumsum(kv_blocks, 0) - kv_blocks
    state_next = state_after[None] + qdo_local[None] - jnp.cumsum(qdo_blocks, 0)
    grad_query, grad_key, grad_value = lax.map(
        block_grads,
        (query_heads, key_heads, value_heads, grad_heads, block_scales, state_prev, state_next),
    )
    grad_query = grad_query.reshape(length, model_width)
    grad_key = grad_key.reshape(length, model_width)
    grad_value = grad_value.reshape(length, model_width)
    head_rows = grad_key[: TAPS - 1]
    wrapped_back = shifted(head_rows, "seq", -1)
    across_back = from_behind(wrapped_back, "outer", -1)
    behind = jnp.where(seq_place == seq_count - 1, across_back, wrapped_back)
    key_grad32 = grad_key.astype(jnp.float32)
    extended = jnp.concatenate([grad_key, behind], 0).astype(jnp.float32)
    grad_pre = jnp.zeros((length, model_width), jnp.float32)
    tap_grads = []
    for tap_index in range(TAPS):
        grad_pre = grad_pre + taps[tap_index] * extended[tap_index : tap_index + length]
        tap_grads.append(
            jnp.sum(key_grad32 * padded[TAPS - 1 - tap_index : TAPS - 1 - tap_index + length], 0)
        )
    grad_pre = grad_pre.astype(jnp.bfloat16)
    conv_local = jnp.stack(tap_grads, 0)
    contract = (((1,), (1,)), ((), ()))
    grad_inputs = lax.dot_general(grad_query, w_query, contract, preferred_element_type=jnp.float32)
    grad_inputs = grad_inputs + lax.dot_general(
        grad_pre, w_key, contract, preferred_element_type=jnp.float32
    )
    grad_inputs = grad_inputs + lax.dot_general(
        grad_value, w_value, contract, preferred_element_type=jnp.float32
    )
    grad_inputs = grad_inputs.astype(jnp.bfloat16)
    over_rows = (((0,), (0,)), ((), ()))
    local_wq = lax.dot_general(inputs, grad_query, over_rows, preferred_element_type=jnp.float32)
    local_wk = lax.dot_general(inputs, grad_pre, over_rows, preferred_element_type=jnp.float32)
    local_wv = lax.dot_general(inputs, grad_value, over_rows, preferred_element_type=jnp.float32)
    grad_wq, grad_wk, grad_wv, grad_conv = lax.psum(
        (local_wq, local_wk, local_wv, conv_local), ("seq", "outer")
    )
    return (grad_inputs, grad_wq, grad_wk, grad_wv, grad_conv)


def solution(mesh):
    in_specs = (
        P(("grp", "outer", "seq"), None),
        P(("grp", "outer", "seq"), None),
        P(),
        P(),
        P(),
        P(),
    )
    out_specs = (
        P(("grp", "outer", "seq"), None),
        P("grp", None),
        P("grp", None),
        P("grp", None),
        P("grp", None),
    )
    return jax.shard_map(
        on_device, mesh=mesh, in_specs=in_specs, out_specs=out_specs, check_vma=False
    )
```

profile of v0, /device:TPU:0, one launch (start us, length us, event | category | flops | bytes accessed | tf_op | source)
XLA Modules:
  0.0 333.5 jit_solution(12223095739537456281)
XLA Ops:
  11.1 3.0 collective-permute-start
  26.5 15.4 %all-gather.3 = bf16[32,64,64]{2,1,0:T(8,128)(2,1)S(1)} all-gather(bf16[8,64,64]{2,1,0:T(8,128)(2,1)S(1)} %convert_element_type.173), channel_id=5, replica_groups=mesh['grp'=2,'seq'=4,'outer'=4] {'seq'}, dimensions={0}, use_global_device_ids=true | all-gather | bytes 327680 | tf_op jit(solution)/shard_map/all_gather | solution.py:30
  42.2 2.8 convolution_convert_fusion.1
  47.6 2.8 reshape.137
  56.1 3.9 %reshape.135 = bf16[2,512,8,64]{3,2,1,0:T(8,128)(2,1)} reshape(bf16[1024,512]{1,0:T(8,128)(2,1)} %add_convert_fusion.1) | data formatting | bytes 2097152 | tf_op jit(solution)/shard_map/reshape | solution.py:100
  60.0 3.3 copy.50
  66.8 16.7 %all-gather.1 = bf16[32,64,64]{2,1,0:T(8,128)(2,1)} all-gather(bf16[8,64,64]{2,1,0:T(8,128)(2,1)S(1)} %convert_element_type.168), channel_id=3, replica_groups=mesh['grp'=2,'seq'=4,'outer'=4] {'seq'}, dimensions={0}, use_global_device_ids=true | all-gather | bytes 327680 | tf_op jit(solution)/shard_map/all_gather | solution.py:30
  83.5 29.6 %all-reduce.6 = (bf16[8,64,64]{2,1,0:T(8,128)(2,1)}, bf16[8,64,64]{2,1,0:T(8,128)(2,1)S(1)}) all-reduce(f32[8,64,64]{2,1,0:T(8,128)} %copy-done.16, f32[8,64,64]{2,1,0:T(8,128)S(1)} %get-tuple-element.348), channel_id=1, replica_groups=mesh['grp'=2,'seq'=4,'outer'=4] {'seq'}, use_global_device_ids=true, to_apply=%region_1.2 | all-reduce | flops 65536 | bytes 393216 | tf_op jit(solution)/shard_map/psum | solution.py:115
  113.2 7.2 %all-gather = bf16[32,64,64]{2,1,0:T(8,128)(2,1)} all-gather(bf16[8,64,64]{2,1,0:T(8,128)(2,1)} %get-tuple-element.338), channel_id=2, replica_groups=mesh['grp'=2,'seq'=4,'outer'=4] {'outer'}, dimensions={0}, use_global_device_ids=true | all-gather | bytes 327680 | tf_op jit(solution)/shard_map/all_gather | solution.py:30
  121.1 10.4 %all-gather.2 = bf16[32,64,64]{2,1,0:T(8,128)(2,1)} all-gather(bf16[8,64,64]{2,1,0:T(8,128)(2,1)S(1)} %get-tuple-element.339), channel_id=4, replica_groups=mesh['grp'=2,'seq'=4,'outer'=4] {'outer'}, dimensions={0}, use_global_device_ids=true | all-gather | bytes 327680 | tf_op jit(solution)/shard_map/all_gather | solution.py:30
  132.2 5.1 %while.60 = (s32[]{:T(128)}, f32[8,64,64]{2,1,0:T(8,128)}, s32[]{:T(128)}, bf16[4,8,64,64]{3,2,1,0:T(8,128)(2,1)}, s32[]{:T(128)}, /*index=5*/s32[]{:T(128)}, s32[]{:T(128)}, s32[]{:T(128)}) while((s32[]{:T(128)}, f32[8,64,64]{2,1,0:T(8,128)}, s32[]{:T(128)}, bf16[4,8,64,64]{3,2,1,0:T(8,128)(2,1)}, s32[]{:T(128)}, /*index=5*/s32[]{:T(128)}, ...), condition=%wide.region_10.11_spmd, body=%wide.region_9.10_spmd.sunk | while | flops 65542 | bytes 327823 | solution.py:37
  141.6 59.3 %while.62 = (s32[]{:T(128)}, bf16[2,512,512]{2,1,0:T(8,128)(2,1)}, bf16[2,512,512]{2,1,0:T(8,128)(2,1)}, bf16[2,512,512]{2,1,0:T(8,128)(2,1)}, bf16[2,512,8,64]{...) while((s32[]{:T(128)}, bf16[2,512,512]{2,1,0:T(8,128)(2,1)}, ...), condition=%wide.region_15.16_spmd, body=%wide.region_14.15_spmd.sunk | while | flops 1960837120 | bytes 65027896 | solution.py:123
  141.7 3.0 select_convert_fusion.6
  152.6 4.6 %fusion.130 = f32[8,64,512]{2,1,0:T(8,128)} fusion(f32[512]{0:T(512)S(1)} %bitcast.174, pred[512,512]{1,0:T(8,128)(4,1)S(1)} %iota_compare_fusion.2, bf16[2,512,8,64]{1,3,2,0:T(8,128)(2,1)} %get-tuple-element.648, s32[]{:T(128)S(6)} %copy.116, bf16[2,512,8,64]{1,3,2,0:T(8,128)(2,1)} %get-tuple-element.644, bf16[2,512,8,64]{1,3,2,0:T(8,128)(2,1)} %get-tuple-element.643), kind=kOutput, calls=%fused_computation.6.clone.1 | convolution fusion | flops 543162368 | bytes 2887168 | tf_op jit(solution)/shard_map/while/body/eval_jaxpr/hts,thj->shj/dot_general | solution.py:63
  157.2 2.9 fusion.131
  162.2 3.3 fusion.132
  171.3 3.0 select_convert_fusion.6
  182.3 4.6 %fusion.130 = f32[8,64,512]{2,1,0:T(8,128)} fusion(f32[512]{0:T(512)S(1)} %bitcast.174, pred[512,512]{1,0:T(8,128)(4,1)S(1)} %iota_compare_fusion.2, bf16[2,512,8,64]{1,3,2,0:T(8,128)(2,1)} %get-tuple-element.648, s32[]{:T(128)S(6)} %copy.116, bf16[2,512,8,64]{1,3,2,0:T(8,128)(2,1)} %get-tuple-element.644, bf16[2,512,8,64]{1,3,2,0:T(8,128)(2,1)} %get-tuple-element.643), kind=kOutput, calls=%fused_computation.6.clone.1 | convolution fusion | flops 543162368 | bytes 2887168 | tf_op jit(solution)/shard_map/while/body/eval_jaxpr/hts,thj->shj/dot_general | solution.py:63
  186.9 2.9 fusion.131
  191.8 3.3 fusion.132
  201.6 5.2 %collective-permute-start.2 = (bf16[3,512]{1,0:T(4,128)(2,1)S(1)}, bf16[3,512]{1,0:T(4,128)(2,1)S(1)}, u32[]{:S(2)}, u32[]{:S(2)}) collective-permute-start(bf16[3,512]{1,0:T(4,128)(2,1)S(1)} %slice.73), channel_id=1, source_target_pairs={{0,12},{4,0},{8,4},{12,8},{1,13},{5,1},{9,5},{13,9},{2,14},{6,2},{... | collective-permute-start | bytes 9224 | tf_op jit(solution)/shard_map/ppermute | solution.py:17
  206.8 3.0 convolution_bitcast_fusion.2
  219.5 32.9 %psum.47 = f32[4,512]{1,0:T(4,128)} all-reduce(f32[4,512]{1,0:T(4,128)S(1)} %pad_maximum_fusion), channel_id=1, replica_groups=mesh['grp'=2,'seq'=4,'outer'=4] {'seq','outer'}, use_global_device_ids=true, to_apply=%region_23.24 | all-reduce | flops 2048 | bytes 16384 | tf_op jit(solution)/shard_map/psum | solution.py:158
  257.6 63.7 %all-reduce.5.cloned.1.call-done = (f32[512,512]{0,1:T(8,128)}, f32[512,512]{0,1:T(8,128)}, f32[512,512]{0,1:T(8,128)}) async-done(((f32[512,512]{0,1:T(8,128)}, f32[512,512]{0,1:T(8,128)}, f32[512,512]{0,1:T(8,128)}), (f32[512,512]{0,1:T(8,128)}, f32[512,512]{0,1:T(8,128)}, f32[512,512]{0,1:T(8,128)})) %all-reduce.5.cloned.1.call-update) | async-done | bytes 3145744 | tf_op jit(solution)/shard_map/psum | solution.py:158
  (168 shorter events, 91.4 us)
Async XLA Ops:
  7.2 7.0 %copy-start.19 = (bf16[1024,512]{1,0:T(8,128)(2,1)S(1)}, bf16[1024,512]{1,0:T(8,128)(2,1)}, u32[]{:S(2)}) copy-start(bf16[1024,512]{1,0:T(8,128)(2,1)} %param.17) | copy-start | bytes 3145732
  7.2 314.2 %all-reduce.5.cloned.1.call-start = ((), (), s32[]{:S(2)}) async-start(), calls=%async_computation | async-start | bytes 6291456 | tf_op jit(solution)/shard_map/psum | solution.py:158
  11.1 33.9 %collective-permute-start = (bf16[3,512]{1,0:T(4,128)(2,1)S(1)}, bf16[3,512]{1,0:T(4,128)(2,1)S(1)}, u32[]{:S(2)}, u32[]{:S(2)}) collective-permute-start(bf16[3,512]{1,0:T(4,128)(2,1)S(1)} %slice.65), channel_id=1, source_target_pairs={{0,4},{4,8},{8,12},{12,0},{1,5},{5,9},{9,13},{13,1},{2,6},{6,10},{... | collective-permute-start | bytes 9224 | tf_op jit(solution)/shard_map/ppermute | solution.py:17
  18.7 5.6 %copy-start.3 = (bf16[2,512,8,64]{1,3,2,0:T(8,128)(2,1)}, bf16[2,512,8,64]{1,3,2,0:T(8,128)(2,1)S(1)}, u32[]{:S(2)}) copy-start(bf16[2,512,8,64]{1,3,2,0:T(8,128)(2,1)S(1)} %copy.51) | copy-start | bytes 3145732
  18.8 5.3 %copy-start.26 = (f32[2,512]{1,0:T(2,128)}, f32[2,512]{1,0:T(2,128)S(1)}, u32[]{:S(2)}) copy-start(f32[2,512]{1,0:T(2,128)S(1)} %multiply_divide_fusion) | copy-start | bytes 12292
  26.5 57.1 %copy-start.14 = (f32[8,64,64]{2,1,0:T(8,128)}, f32[8,64,64]{2,1,0:T(8,128)S(1)}, u32[]{:S(2)}) copy-start(f32[8,64,64]{2,1,0:T(8,128)S(1)} %get-tuple-element.348) | copy-start | bytes 393220
  42.2 5.4 %copy-start.8 = (f32[8,64,64]{2,1,0:T(8,128)}, f32[8,64,64]{2,1,0:T(8,128)S(1)}, u32[]{:S(2)}) copy-start(f32[8,64,64]{2,1,0:T(8,128)S(1)} %get-tuple-element.225) | copy-start | bytes 393220
  42.2 4.1 %copy-start.36 = (bf16[4,512]{1,0:T(4,128)(2,1)S(1)}, bf16[4,512]{1,0:T(4,128)(2,1)}, u32[]{:S(2)}) copy-start(bf16[4,512]{1,0:T(4,128)(2,1)} %param.21) | copy-start | bytes 12292
  45.0 7.6 %collective-permute-start.1 = (bf16[3,512]{1,0:T(4,128)(2,1)S(1)}, bf16[3,512]{1,0:T(4,128)(2,1)S(1)}, u32[]{:S(2)}, u32[]{:S(2)}) collective-permute-start(bf16[3,512]{1,0:T(4,128)(2,1)S(1)} %collective-permute-done), channel_id=1, source_target_pairs={{0,1},{1,2},{2,3},{4,5},{5,6},{6,7},{8,9},{9,10},{10,11},{12,13},{... | collective-permute-start | bytes 9224 | tf_op jit(solution)/shard_map/ppermute | solution.py:23
  46.3 7.8 %copy-start.28 = (f32[1,512]{1,0:T(1,128)}, f32[1,512]{1,0:T(1,128)S(1)}, u32[]{:S(2)}) copy-start(f32[1,512]{1,0:T(1,128)S(1)} %get-tuple-element.342) | copy-start | bytes 6148
  46.3 7.8 %copy-start.30 = (f32[1,512]{1,0:T(1,128)}, f32[1,512]{1,0:T(1,128)S(1)}, u32[]{:S(2)}) copy-start(f32[1,512]{1,0:T(1,128)S(1)} %get-tuple-element.343) | copy-start | bytes 6148
  46.4 7.8 %copy-start.32 = (f32[1,512]{1,0:T(1,128)}, f32[1,512]{1,0:T(1,128)S(1)}, u32[]{:S(2)}) copy-start(f32[1,512]{1,0:T(1,128)S(1)} %get-tuple-element.344) | copy-start | bytes 6148
  46.4 7.8 %copy-start.34 = (f32[1,512]{1,0:T(1,128)}, f32[1,512]{1,0:T(1,128)S(1)}, u32[]{:S(2)}) copy-start(f32[1,512]{1,0:T(1,128)S(1)} %get-tuple-element.345) | copy-start | bytes 6148
  137.4 3.4 %copy-start.17 = (f32[2,8,64,64]{3,2,1,0:T(8,128)S(1)}, f32[2,8,64,64]{3,2,1,0:T(8,128)}, u32[]{:S(2)}) copy-start(f32[2,8,64,64]{3,2,1,0:T(8,128)} %get-tuple-element.349) | copy-start | bytes 786436
  162.2 3.3 copy-start.5
  162.2 3.3 copy-start.6
  191.8 3.3 copy-start.5
  191.8 3.3 copy-start.6
  201.6 8.3 %collective-permute-start.2 = (bf16[3,512]{1,0:T(4,128)(2,1)S(1)}, bf16[3,512]{1,0:T(4,128)(2,1)S(1)}, u32[]{:S(2)}, u32[]{:S(2)}) collective-permute-start(bf16[3,512]{1,0:T(4,128)(2,1)S(1)} %slice.73), channel_id=1, source_target_pairs={{0,12},{4,0},{8,4},{12,8},{1,13},{5,1},{9,5},{13,9},{2,14},{6,2},{... | collective-permute-start | bytes 9224 | tf_op jit(solution)/shard_map/ppermute | solution.py:17
  206.8 4.3 %copy-start.22 = (bf16[2,512,512]{2,1,0:T(8,128)(2,1)S(1)}, bf16[2,512,512]{2,1,0:T(8,128)(2,1)}, u32[]{:S(2)}) copy-start(bf16[2,512,512]{2,1,0:T(8,128)(2,1)} %get-tuple-element.228) | copy-start | bytes 3145732
  209.8 3.0 collective-permute-start.3
  219.5 35.0 %copy-start.13 = (bf16[1024,512]{1,0:T(8,128)(2,1)S(1)}, bf16[1024,512]{1,0:T(8,128)(2,1)}, u32[]{:S(2)}) copy-start(bf16[1024,512]{1,0:T(8,128)(2,1)} %copy-done.12) | copy-start | bytes 3145732
  219.5 35.0 %copy-start.24 = (bf16[512,512]{1,0:T(8,128)(2,1)S(1)}, bf16[512,512]{1,0:T(8,128)(2,1)}, u32[]{:S(2)}) copy-start(bf16[512,512]{1,0:T(8,128)(2,1)} %param.19) | copy-start | bytes 1572868
  321.4 4.0 %copy-start.20 = (f32[512,512]{0,1:T(8,128)S(1)}, f32[512,512]{0,1:T(8,128)}, u32[]{:S(2)}) copy-start(f32[512,512]{0,1:T(8,128)} %get-tuple-element.337) | copy-start | bytes 3145732
  (24 other events, 45.8 us)
Sparse Core Ops, SparseCore 0:
  217.3 104.0 all-reduce.4
where the time goes:
time: 335 us; the launch traced here: 334 us
  blocking collectives  112 us (33%)
  waiting for transfers between devices  63.8 us (19%)
  matrix products  58.5 us (17%)
  local copies, waits for them, and re-layouts  56.5 us (17%)
  other arithmetic  16.9 us (5%)
  between operations  14.5 us (4%)
  starting transfers between devices  10.8 us (3%)
    psum x1, waiting for transfers between devices, on_device(): lax.psum((local_wq, local_wk, local_wv, conv_local), ('seq', 'outer'))  63.7 us
    all_gather x4, blocking collectives, entering(): gathered = lax.all_gather(x.astype(jnp.bfloat16), axis)  49.7 us
    psum x1, blocking collectives, on_device(): lax.psum((local_wq, local_wk, local_wv, conv_local), ('seq', 'outer'))  32.9 us
    psum x1, blocking collectives, on_device(): kv_group, qdo_group = lax.psum((kv_local, qdo_local), 'seq')  29.6 us
    dynamic_update_slice x10, local copies, waits for them, and re-layouts, on_device(): lax.map(block_grads, (query_heads, key_heads, value_heads, grad_heads, bl...  20.6 us
    unnamed x66, local copies, waits for them, and re-layouts  10.2 us
    dot_general x2, matrix products, block_grads(): jnp.einsum('hts,thj->shj', mixing, grad_rows, preferred_element_type=jnp....  9.25 us
    while x4, local copies, waits for them, and re-layouts, on_device(): lax.map(block_grads, (query_heads, key_heads, value_heads, grad_heads, bl...  9.23 us
  transfers between devices with their start and end apart: 5, of which 1 were waited for; matrix products, arithmetic and copies ran while one was open for 10% of the time, Pallas kernels for 0%

commit v1 on v0

v1 whole, which is shorter than its diff:
```python
import functools
import math

import jax
import jax.numpy as jnp
from jax import lax
from jax.experimental import pallas as pl
from jax.experimental.pallas import tpu as pltpu
from jax.sharding import PartitionSpec as P

D = 512
HEADS = 8
HEAD_DIM = 64
TAPS = 4
BLOCK = 512
HALF = BLOCK // 2
TILE = 256
PAIR = 2 * HEAD_DIM
PAIRS = D // PAIR
OWNERS = 16
SLICE = PAIRS * HEAD_DIM // OWNERS
EDGE = 16
MESH = pl.DeviceIdType.MESH
BF = jnp.bfloat16
F32 = jnp.float32

NN = (((1,), (0,)), ((), ()))
NT = (((1,), (1,)), ((), ()))
TN = (((0,), (0,)), ((), ()))


def mm(a, b, dims):
    return lax.dot_general(a, b, dims, preferred_element_type=F32)


def kernel(
    seq_count, outer_count,
    inp, go, wq, wk, wv, taps_ref,
    gin, out, conv_out,
    kp32, q, qs, k, v, gs, xt, gva, gq, gk32, gv, gp,
    edge_k, edge_kr, edge_g, edge_gr,
    kvb, qdb, sb, rb, so, st, sp, sn,
    wb, rc, sx, rx, sz, rz, cown, crecv,
    edge_sem, s1_send, s1_recv, s2_send, s2_recv, cv_send, cv_recv,
    c_sem, x_send, x_recv, z_send, z_recv, az_send, az_recv, ax_send, ax_recv, ac_sem,
):
    Z = seq_count
    X = outer_count // 2
    N = seq_count * outer_count
    length = inp.shape[0]
    blocks = length // BLOCK
    tiles = length // TILE
    steps = blocks * PAIRS
    r = D // N
    z = lax.axis_index("seq")
    o = lax.axis_index("outer")
    x, core = o // 2, o % 2
    me = o * Z + z

    def at(place):
        return {"seq": place % Z, "outer": place // Z}

    def others(count, mine, body):
        def one(i, carry):
            @pl.when(i != mine)
            def _():
                body(i)
            return carry
        lax.fori_loop(0, count, one, 0)

    def remote(src, dst, send, recv, device):
        return pltpu.make_async_remote_copy(
            src_ref=src, dst_ref=dst, send_sem=send, recv_sem=recv,
            device_id=device, device_id_type=MESH,
        )

    barrier = pltpu.get_barrier_semaphore()
    others(N, me, lambda i: pl.semaphore_signal(
        barrier, inc=1, device_id=at(i), device_id_type=MESH))

    lane = lax.broadcasted_iota(jnp.int32, (1, PAIR), 1)
    low = jnp.where(lane < HEAD_DIM, 1.0, 0.0)
    high = 1.0 - low
    masks = (low.astype(BF), high.astype(BF))

    def keys_tile(i, carry):
        rows = pl.ds(pl.multiple_of(i * TILE, TILE), TILE)
        res = mm(inp[rows, :], wk[...], NN).astype(BF).astype(F32)
        kp32[pl.ds(pl.multiple_of(i * TILE + 8, 8), TILE), :] = res
        return carry

    lax.fori_loop(0, tiles, keys_tile, 0)
    edge_k[...] = kp32[8 + length - EDGE : 8 + length, :].astype(BF)

    pl.semaphore_wait(barrier, N - 1)
    after, ahead = (me + 1) % N, (me + N - 1) % N
    send_k = remote(edge_k, edge_kr, edge_sem.at[0], edge_sem.at[1], at(after))
    send_k.start()

    def rest_tile(i, carry):
        start = pl.multiple_of(i * TILE, TILE)
        rows = pl.ds(start, TILE)
        place = lax.broadcasted_iota(jnp.int32, (TILE, 128), 0) + (me * length + start)
        scale = 1.0 / (jnp.sqrt(place.astype(F32) + 1.0) * math.sqrt(HEAD_DIM))
        scale = jnp.concatenate([scale] * (D // 128), 1)
        block = inp[rows, :]
        queries = mm(block, wq[...], NN).astype(BF)
        q[rows, :] = queries
        qs[rows, :] = (queries.astype(F32) * scale).astype(BF)
        v[rows, :] = mm(block, wv[...], NN).astype(BF)
        gs[rows, :] = (go[rows, :].astype(F32) * scale).astype(BF)
        xt[:, rows] = block.T
        return carry

    lax.fori_loop(0, tiles, rest_tile, 0)
    taps = taps_ref[...].astype(F32)
    send_k.wait()
    keep = jnp.where(me == 0, 0.0, 1.0)
    kp32[0:8, :] = edge_kr[EDGE - 8 : EDGE, :].astype(F32) * keep

    def conv_tile(i, carry):
        start = pl.multiple_of(i * TILE, TILE)
        rows = kp32[pl.ds(start, TILE + 8), :]
        total = taps[0:1] * rows[8 : 8 + TILE]
        for j in range(1, TAPS):
            total = total + taps[j : j + 1] * rows[8 - j : 8 - j + TILE]
        k[pl.ds(start, TILE), :] = total.astype(BF)
        return carry

    lax.fori_loop(0, tiles, conv_tile, 0)

    def shrink(full):
        return full[:HEAD_DIM] * low + full[HEAD_DIM:] * high

    for p in range(PAIRS):
        cols = slice(p * PAIR, (p + 1) * PAIR)
        kv_sum = qd_sum = None
        for b in range(blocks):
            rows = slice(b * BLOCK, (b + 1) * BLOCK)
            kv = shrink(mm(k[rows, cols], v[rows, cols], TN))
            qd = shrink(mm(qs[rows, cols], go[rows, cols], TN))
            kvb[b, p] = kv
            qdb[b, p] = qd
            kv_sum = kv if kv_sum is None else kv_sum + kv
            qd_sum = qd if qd_sum is None else qd_sum + qd
        per = HEAD_DIM // SLICE
        for u in range(per):
            sb[p * per + u, 0] = kv_sum[u * SLICE : (u + 1) * SLICE].astype(BF)
            sb[p * per + u, 1] = qd_sum[u * SLICE : (u + 1) * SLICE].astype(BF)

    def to_owner(i):
        return remote(sb.at[i], rb.at[me], s1_send.at[i], s1_recv.at[me], at(i))

    def from_member(i):
        return remote(sb.at[0], rb.at[i], s1_send.at[0], s1_recv.at[i], at(i))

    def to_member(i):
        return remote(so.at[i], st.at[me], s2_send.at[i], s2_recv.at[me], at(i))

    def from_owner(i):
        return remote(so.at[0], st.at[i], s2_send.at[0], s2_recv.at[i], at(i))

    def as_owner(body):
        if N > OWNERS:
            pl.when(me < OWNERS)(body)
        else:
            body()

    others(OWNERS, me, lambda i: to_owner(i).start())

    def attend(first, second, third, keys_first, index):
        b, p = index // PAIRS, index % PAIRS
        lanes = pl.ds(pl.multiple_of(p * PAIR, PAIR), PAIR)
        base = b * BLOCK
        lo = pl.ds(pl.multiple_of(base, HALF), HALF)
        hi = pl.ds(pl.multiple_of(base + HALF, HALF), HALF)
        row = lax.broadcasted_iota(jnp.int32, (HALF, HALF), 0)
        col = lax.broadcasted_iota(jnp.int32, (HALF, HALF), 1)
        causal = row <= col if keys_first else row >= col
        a_lo, a_hi = first[lo, lanes], first[hi, lanes]
        b_lo, b_hi = second[lo, lanes], second[hi, lanes]
        c_lo, c_hi = third[lo, lanes], third[hi, lanes]
        res_lo = res_hi = None
        for mask in masks:
            al, ah = a_lo * mask, a_hi * mask
            cl, ch = c_lo * mask, c_hi * mask
            s_ll = jnp.where(causal, mm(al, b_lo, NT), 0.0).astype(BF)
            s_hh = jnp.where(causal, mm(ah, b_hi, NT), 0.0).astype(BF)
            if keys_first:
                s_x = mm(al, b_hi, NT).astype(BF)
                one_lo = mm(s_ll, cl, NN) + mm(s_x, ch, NN)
                one_hi = mm(s_hh, ch, NN)
            else:
                s_x = mm(ah, b_lo, NT).astype(BF)
                one_lo = mm(s_ll, cl, NN)
                one_hi = mm(s_hh, ch, NN) + mm(s_x, cl, NN)
            res_lo = one_lo if res_lo is None else res_lo + one_lo
            res_hi = one_hi if res_hi is None else res_hi + one_hi
        return b, p, lanes, lo, hi, res_lo, res_hi

    def value_step(index, carry):
        _, _, lanes, lo, hi, res_lo, res_hi = attend(k, qs, go, True, index)
        gva[lo, lanes] = res_lo
        gva[hi, lanes] = res_hi
        return carry

    half = PAIRS * (blocks // 2)
    lax.fori_loop(0, half, value_step, 0)

    @as_owner
    def _():
        others(N, me, lambda i: from_member(i).wait_recv())
        rb[me] = sb[me]

        def prefix(i, carry):
            so[i, 0] = carry.astype(BF)
            return carry + rb[i, 0].astype(F32)

        lax.fori_loop(0, N, prefix, jnp.zeros((SLICE, PAIR), F32))

        def suffix(i, carry):
            so[N - 1 - i, 1] = carry.astype(BF)
            return carry + rb[N - 1 - i, 1].astype(F32)

        lax.fori_loop(0, N, suffix, jnp.zeros((SLICE, PAIR), F32))
        st[me] = so[me]
        others(N, me, lambda i: to_member(i).start())

    lax.fori_loop(half, steps, value_step, 0)
    others(OWNERS, me, lambda i: from_owner(i).wait_recv())

    per = HEAD_DIM // SLICE
    for p in range(PAIRS):
        prev = st[p * per : (p + 1) * per, 0].astype(F32).reshape(HEAD_DIM, PAIR)
        for b in range(blocks):
            sp[b, p] = jnp.concatenate([prev * low, prev * high], 0).astype(BF)
            prev = prev + kvb[b, p]
        later = st[p * per : (p + 1) * per, 1].astype(F32).reshape(HEAD_DIM, PAIR)
        for b in reversed(range(blocks)):
            sn[b, p] = jnp.concatenate([later * low, later * high], 0).astype(BF)
            later = later + qdb[b, p]

    def value_finish(index, carry):
        b, p = index // PAIRS, index % PAIRS
        lanes = pl.ds(pl.multiple_of(p * PAIR, PAIR), PAIR)
        rows = pl.ds(pl.multiple_of(b * BLOCK, BLOCK), BLOCK)
        gv[rows, lanes] = (gva[rows, lanes] + mm(k[rows, lanes], sn[b, p], NN)).astype(BF)
        return carry

    lax.fori_loop(0, steps, value_finish, 0)

    def weight(c, grads):
        for h in range(2):
            res = mm(xt[h * HALF : (h + 1) * HALF, :], grads[...], NN).astype(BF)
            for i in range(X * Z):
                wb[c, h, i // Z, i % Z] = res[r * i : r * i + r]

    def core_copy(c):
        return remote(wb.at[c, 1 - core], rc.at[c], c_sem.at[c, 0], c_sem.at[c, 1],
                      {"outer": x * 2 + 1 - core})

    def x_copy(c, i, source):
        return remote(sx.at[c, i], rx.at[c, source], x_send.at[c, i], x_recv.at[c, source],
                      {"outer": i * 2 + core})

    def z_copy(c, i, source):
        return remote(sz.at[c, i], rz.at[c, source], z_send.at[c, i], z_recv.at[c, source],
                      {"seq": i})

    def az_copy(c, i, source):
        slot = out.at[c, core, x, source]
        return remote(slot, slot, az_send.at[c, i], az_recv.at[c, source], {"seq": i})

    def ax_copy(c, i, source):
        slot = out.at[c, core, source]
        return remote(slot, slot, ax_send.at[c, i], ax_recv.at[c, source],
                      {"outer": i * 2 + core})

    def ac_copy(c, source):
        slot = out.at[c, source]
        return remote(slot, slot, ac_sem.at[c, 0], ac_sem.at[c, 1],
                      {"outer": x * 2 + 1 - core})

    def stage_core(c):
        core_copy(c).start()

    def stage_x(c):
        core_copy(c).wait_recv()
        for i in range(X):
            sx[c, i] = (wb[c, core, i].astype(F32) + rc[c, i].astype(F32)).astype(BF)
        others(X, x, lambda i: x_copy(c, i, x).start())

    def stage_z(c):
        others(X, x, lambda i: x_copy(c, i, i).wait_recv())
        rx[c, x] = sx[c, x]
        total = rx[c, 0].astype(F32)
        for i in range(1, X):
            total = total + rx[c, i].astype(F32)
        sz[c] = total.astype(BF)
        others(Z, z, lambda i: z_copy(c, i, z).start())

    def stage_az(c):
        others(Z, z, lambda i: z_copy(c, i, i).wait_recv())
        rz[c, z] = sz[c, z]
        total = rz[c, 0].astype(F32)
        for i in range(1, Z):
            total = total + rz[c, i].astype(F32)
        out[c, core, x, z] = total.astype(BF)
        others(Z, z, lambda i: az_copy(c, i, z).start())

    def stage_ax(c):
        others(Z, z, lambda i: az_copy(c, i, i).wait_recv())
        others(X, x, lambda i: ax_copy(c, i, x).start())

    def stage_ac(c):
        others(X, x, lambda i: ax_copy(c, i, i).wait_recv())
        ac_copy(c, core).start()

    def stage_end(c):
        ac_copy(c, 1 - core).wait_recv()
        core_copy(c).wait_send()
        others(X, x, lambda i: x_copy(c, i, x).wait_send())
        others(Z, z, lambda i: z_copy(c, i, z).wait_send())
        others(Z, z, lambda i: az_copy(c, i, z).wait_send())
        others(X, x, lambda i: ax_copy(c, i, x).wait_send())
        ac_copy(c, core).wait_send()

    weight(0, gv)
    stage_core(0)

    def query_step(index, carry):
        b, p, lanes, lo, hi, res_lo, res_hi = attend(gs, v, k, False, index)
        state = sp[b, p]
        gq[lo, lanes] = (res_lo + mm(gs[lo, lanes], state, NT)).astype(BF)
        gq[hi, lanes] = (res_hi + mm(gs[hi, lanes], state, NT)).astype(BF)
        return carry

    lax.fori_loop(0, half, query_step, 0)
    stage_x(0)
    lax.fori_loop(half, steps, query_step, 0)
    weight(1, gq)
    stage_core(1)
    stage_z(0)

    def key_step(index, carry):
        b, p, lanes, lo, hi, res_lo, res_hi = attend(v, gs, q, True, index)
        state = sn[b, p]
        gk32[lo, lanes] = (res_lo + mm(v[lo, lanes], state, NT)).astype(BF).astype(F32)
        gk32[hi, lanes] = (res_hi + mm(v[hi, lanes], state, NT)).astype(BF).astype(F32)
        return carry

    lax.fori_loop(0, half, key_step, 0)
    edge_g[...] = gk32[0:EDGE, :].astype(BF)
    send_g = remote(edge_g, edge_gr, edge_sem.at[2], edge_sem.at[3], at(ahead))
    send_g.start()
    stage_x(1)
    stage_az(0)
    lax.fori_loop(half, steps, key_step, 0)
    stage_z(1)
    stage_ax(0)

    send_g.wait()
    keep_g = jnp.where(me == N - 1, 0.0, 1.0)
    gk32[length : length + 8, :] = edge_gr[0:8, :].astype(F32) * keep_g

    def pre_tile(i, sums):
        start = pl.multiple_of(i * TILE, TILE)
        rows = gk32[pl.ds(start, TILE + 8), :]
        keys = kp32[pl.ds(start, TILE + 8), :]
        own = rows[0:TILE]
        total = taps[0:1] * own
        for j in range(1, TAPS):
            total = total + taps[j : j + 1] * rows[j : j + TILE]
        gp[pl.ds(start, TILE), :] = total.astype(BF)
        return tuple(
            sums[j] + jnp.sum((own * keys[8 - j : 8 - j + TILE]).reshape(TILE // 8, 8, D), 0)
            for j in range(TAPS)
        )

    sums = lax.fori_loop(0, tiles, pre_tile, tuple(jnp.zeros((8, D), F32) for _ in range(TAPS)))
    for j in range(TAPS):
        cown[j : j + 1, :] = jnp.sum(sums[j], 0, keepdims=True)

    def conv_copy(i, source):
        return remote(cown, crecv.at[source], cv_send.at[i], cv_recv.at[source], at(i))

    weight(2, gp)
    stage_core(2)
    stage_ac(0)
    stage_az(1)
    others(N, me, lambda i: conv_copy(i, me).start())

    def gin_tile(i, carry):
        rows = pl.ds(pl.multiple_of(i * TILE, TILE), TILE)
        total = mm(gq[rows, :], wq[...], NT)
        total = total + mm(gp[rows, :], wk[...], NT)
        total = total + mm(gv[rows, :], wv[...], NT)
        gin[rows, :] = total.astype(BF)
        return carry

    stage_x(2)
    lax.fori_loop(0, tiles // 2, gin_tile, 0)
    stage_ax(1)
    stage_z(2)
    lax.fori_loop(tiles // 2, tiles, gin_tile, 0)
    stage_ac(1)
    stage_az(2)
    others(N, me, lambda i: conv_copy(i, i).wait_recv())
    crecv[me] = cown[...]
    conv_out[...] = lax.fori_loop(
        1, N, lambda i, total: total + crecv[i], crecv[0])
    stage_ax(2)
    stage_ac(2)
    others(OWNERS, me, lambda i: to_owner(i).wait_send())

    @as_owner
    def _():
        others(N, me, lambda i: to_member(i).wait_send())

    others(N, me, lambda i: conv_copy(i, me).wait_send())
    stage_end(0)
    stage_end(1)
    stage_end(2)


def on_device(seq_count, outer_count, inputs, grad_out, w_query, w_key, w_value, conv_taps):
    length = inputs.shape[0]
    Z, X = seq_count, outer_count // 2
    N = seq_count * outer_count
    r = D // N
    blocks = length // BLOCK
    vm = pltpu.VMEM
    dma = pltpu.SemaphoreType.DMA
    full = vm((length, D), BF)
    edge = vm((EDGE, D), BF)
    state = vm((blocks, PAIRS, HEAD_DIM, PAIR), F32)
    member = vm((N, 2, SLICE, PAIR), BF)
    owner = vm((OWNERS, 2, SLICE, PAIR), BF)
    square = vm((blocks, PAIRS, PAIR, PAIR), BF)
    scratch = [
        vm((length + 8, D), F32), full, full, full, full, full, vm((D, length), BF),
        vm((length, D), F32), full, vm((length + 8, D), F32), full, full,
        edge, edge, edge, edge,
        state, state, owner, member, member, owner, square, square,
        vm((3, 2, X, Z, r, D), BF), vm((3, X, Z, r, D), BF), vm((3, X, Z, r, D), BF),
        vm((3, X, Z, r, D), BF), vm((3, Z, r, D), BF), vm((3, Z, r, D), BF),
        vm((TAPS, D), F32), vm((N, TAPS, D), F32),
        dma((4,)), dma((OWNERS,)), dma((N,)), dma((N,)), dma((OWNERS,)), dma((N,)), dma((N,)),
        dma((3, 2)), dma((3, X)), dma((3, X)), dma((3, Z)), dma((3, Z)),
        dma((3, Z)), dma((3, Z)), dma((3, X)), dma((3, X)), dma((3, 2)),
    ]
    spec = pl.BlockSpec(memory_space=pltpu.VMEM)
    grad_inputs, weights, grad_conv = pl.pallas_call(
        functools.partial(kernel, seq_count, outer_count),
        out_shape=(
            jax.ShapeDtypeStruct((length, D), BF),
            jax.ShapeDtypeStruct((3, 2, X, Z, r, D), BF),
            jax.ShapeDtypeStruct((TAPS, D), F32),
        ),
        in_specs=[spec] * 6,
        out_specs=(spec, spec, spec),
        scratch_shapes=scratch,
        compiler_params=pltpu.CompilerParams(
            collective_id=0, has_side_effects=True, vmem_limit_bytes=56 * 1024 * 1024
        ),
    )(inputs, grad_out, w_query, w_key, w_value, conv_taps)
    weights = weights.reshape(3, D, D).astype(F32)
    return (grad_inputs, weights[1], weights[2], weights[0], grad_conv)


def solution(mesh):
    rows = P(("grp", "outer", "seq"), None)
    body = functools.partial(on_device, mesh.shape["seq"], mesh.shape["outer"])
    return jax.shard_map(
        body,
        mesh=mesh,
        in_specs=(rows, rows, P(), P(), P(), P()),
        out_specs=(rows, P("grp", None), P("grp", None), P("grp", None), P("grp", None)),
        check_vma=False,
    )
```

time: 335 us -> 74.2 us (0.22)
  blocking collectives: 112 us -> 0 us
  Pallas kernels: 0 us -> 68.6 us
  waiting for transfers between devices: 63.8 us -> 0 us
  matrix products: 58.5 us -> 0 us
  local copies, waits for them, and re-layouts: 56.5 us -> 4.82 us
  other arithmetic: 16.9 us -> 0 us
  between operations: 14.5 us -> 0.65 us
  starting transfers between devices: 10.8 us -> 0 us
    pallas_call x0 -> x1, Pallas kernels: none -> 68.6 us  [on_device(): pl.pallas_call(functools.partial(kernel, seq_count, outer_count), out_sha...]
    psum x1 -> x0, waiting for transfers between devices: 63.7 us -> none  [on_device(): lax.psum((local_wq, local_wk, local_wv, conv_local), ('seq', 'outer'))]
    psum x2 -> x0, blocking collectives: 62.5 us -> none  [the longest x1 32.9 us: on_device(): lax.psum((local_wq, local_wk, local_wv, conv_local), ('seq', 'outer'))]
    dot_general x25 -> x0, matrix products: 58.5 us -> none  [the longest x2 9.25 us: block_grads(): jnp.einsum('hts,thj->shj', mixing, grad_rows, preferred_element_type=jnp....]
    all_gather x4 -> x0, blocking collectives: 49.7 us -> none  [entering(): gathered = lax.all_gather(x.astype(jnp.bfloat16), axis)]
    dynamic_update_slice x10 -> x0, local copies, waits for them, and re-layouts: 20.6 us -> none  [on_device(): lax.map(block_grads, (query_heads, key_heads, value_heads, grad_heads, bl...]
    while x28 -> x0, local copies, waits for them, and re-layouts: 11.6 us -> none  [the longest x4 9.23 us: on_device(): lax.map(block_grads, (query_heads, key_heads, value_heads, grad_heads, bl...]
    ppermute x4 -> x0, starting transfers between devices: 10.8 us -> none  [the longest x2 8.23 us: shifted(): lax.ppermute(x, axis, [(i, (i + by) % devices) for i in range(devices)])]
  transfers between devices with their start and end apart: 5 -> 0, of which waited for: 1 -> 0; matrix products, arithmetic and copies ran while one was open for 10% -> 0% of each run, Pallas kernels for 0% -> 0%
where the time goes in v1:
time: 74.2 us; the launch traced here: 74.1 us
  Pallas kernels  68.6 us (92%)
  local copies, waits for them, and re-layouts  4.82 us (6%)
    pallas_call x1, Pallas kernels, on_device(): pl.pallas_call(functools.partial(kernel, seq_count, outer_count), out_sha...  68.6 us
    slice x1, local copies, waits for them, and re-layouts, on_device(): return (grad_inputs, weights[1], weights[2], weights[0], grad_conv)  3.24 us
    unnamed x6, local copies, waits for them, and re-layouts  1.58 us

profile of v1, /device:TPU:0, one launch (start us, length us, event | category | flops | bytes accessed | tf_op | source)
XLA Modules:
  0.0 74.1 jit_solution(13864578497245735628)
XLA Ops:
  0.6 68.6 %shard_map.101 = (bf16[1024,512]{1,0:T(8,128)(2,1)}, bf16[3,2,2,4,32,512]{5,4,3,2,1,0:T(8,128)(2,1)}, f32[4,512]{1,0:T(4,128)}) custom-call(bf16[1024,512]{1,0:T(8,128)(2,1)} %inp.1, bf16[1024,512]{1,0:T(8,128)(2,1)} %go.1, bf16[512,512]{1,0:T(8,128)(2,1)} %wq.1, bf16[512,512]{1,0:T(8,128)(2,1)} %wk.1, bf16[512,512]{1,0:T(8,128)(2,1)} %wv.1, ...), custom_call_target="tpu_custom_call" | custom-call | tf_op jit(solution)/shard_map/pallas_call | solution.py:453
  69.2 0.0 copy-start
  69.2 3.2 %fusion = (f32[1,2,2,4,32,512]{5,4,3,2,1,0:T(8,128)}, f32[1,2,2,4,32,512]{5,4,3,2,1,0:T(8,128)}, f32[1,2,2,4,32,512]{5,4,3,2,1,0:T(8,128)}) fusion(bf16[3,2,2,4,32,512]{5,4,3,2,1,0:T(8,128)(2,1)} %get-tuple-element.9), kind=kLoop, calls=%fused_computation | loop fusion | bytes 6291456 | tf_op jit(solution)/shard_map/slice | solution.py:468
  72.5 0.0 copy-start.1
  72.5 0.0 copy-done
  72.5 1.0 %copy.13 = bf16[1024,512]{1,0:T(8,128)(2,1)} copy(bf16[1024,512]{1,0:T(8,128)(2,1)S(1)} %copy-done) | data formatting | bytes 2097152
  73.5 0.0 copy-done.1
  73.5 0.6 copy.14
Async XLA Ops:
  69.2 3.3 %copy-start = (bf16[1024,512]{1,0:T(8,128)(2,1)S(1)}, bf16[1024,512]{1,0:T(8,128)(2,1)}, u32[]{:S(2)}) copy-start(bf16[1024,512]{1,0:T(8,128)(2,1)} %get-tuple-element.19) | copy-start | bytes 3145732
  72.5 1.0 %copy-start.1 = (f32[4,512]{1,0:T(4,128)S(1)}, f32[4,512]{1,0:T(4,128)}, u32[]{:S(2)}) copy-start(f32[4,512]{1,0:T(4,128)} %get-tuple-element.23) | copy-start | bytes 24580

commit v2 on v1

--- a/solution.py
+++ b/solution.py
@@ -17,8 +17,6 @@
 TILE = 256
 PAIR = 2 * HEAD_DIM
 PAIRS = D // PAIR
-OWNERS = 16
-SLICE = PAIRS * HEAD_DIM // OWNERS
 EDGE = 16
 MESH = pl.DeviceIdType.MESH
 BF = jnp.bfloat16
@@ -37,11 +35,11 @@
     seq_count, outer_count,
     inp, go, wq, wk, wv, taps_ref,
     gin, out, conv_out,
-    kp32, q, qs, k, v, gs, xt, gva, gq, gk32, gv, gp,
+    kp32, q, qs, k, v, gs, xt, gva, gqa, gq, gk32, gv, gp,
     edge_k, edge_kr, edge_g, edge_gr,
-    kvb, qdb, sb, rb, so, st, sp, sn,
-    wb, rc, sx, rx, sz, rz, cown, crecv,
-    edge_sem, s1_send, s1_recv, s2_send, s2_recv, cv_send, cv_recv,
+    kvb, qdb, sb, rb, part, tot, trecv, so, st, sp, sn,
+    wb, rc, sx, rx, sz, rz, csend, crc, crx, crz,
+    edge_sem, s1_send, s1_recv, t_send, t_recv, s2_send, s2_recv, cv_c, cv_x, cv_z,
     c_sem, x_send, x_recv, z_send, z_recv, az_send, az_recv, ax_send, ax_recv, ac_sem,
 ):
     Z = seq_count
@@ -52,6 +50,7 @@
     tiles = length // TILE
     steps = blocks * PAIRS
     r = D // N
+    rows_z = PAIRS * HEAD_DIM // Z
     z = lax.axis_index("seq")
     o = lax.axis_index("outer")
     x, core = o // 2, o % 2
@@ -75,8 +74,15 @@
         )
 
     barrier = pltpu.get_barrier_semaphore()
-    others(N, me, lambda i: pl.semaphore_signal(
-        barrier, inc=1, device_id=at(i), device_id_type=MESH))
+    after, ahead = (me + 1) % N, (me + N - 1) % N
+
+    def greet(device):
+        pl.semaphore_signal(barrier, inc=1, device_id=device, device_id_type=MESH)
+
+    others(Z, z, lambda i: greet({"seq": i}))
+    others(outer_count, o, lambda i: greet({"outer": i}))
+    greet(at(after))
+    greet(at(ahead))
 
     lane = lax.broadcasted_iota(jnp.int32, (1, PAIR), 1)
     low = jnp.where(lane < HEAD_DIM, 1.0, 0.0)
@@ -92,8 +98,7 @@
     lax.fori_loop(0, tiles, keys_tile, 0)
     edge_k[...] = kp32[8 + length - EDGE : 8 + length, :].astype(BF)
 
-    pl.semaphore_wait(barrier, N - 1)
-    after, ahead = (me + 1) % N, (me + N - 1) % N
+    pl.semaphore_wait(barrier, Z + outer_count)
     send_k = remote(edge_k, edge_kr, edge_sem.at[0], edge_sem.at[1], at(after))
     send_k.start()
 
@@ -109,7 +114,6 @@
         qs[rows, :] = (queries.astype(F32) * scale).astype(BF)
         v[rows, :] = mm(block, wv[...], NN).astype(BF)
         gs[rows, :] = (go[rows, :].astype(F32) * scale).astype(BF)
-        xt[:, rows] = block.T
         return carry
 
     lax.fori_loop(0, tiles, rest_tile, 0)
@@ -143,30 +147,22 @@
             qdb[b, p] = qd
             kv_sum = kv if kv_sum is None else kv_sum + kv
             qd_sum = qd if qd_sum is None else qd_sum + qd
-        per = HEAD_DIM // SLICE
+        per = HEAD_DIM // rows_z
         for u in range(per):
-            sb[p * per + u, 0] = kv_sum[u * SLICE : (u + 1) * SLICE].astype(BF)
-            sb[p * per + u, 1] = qd_sum[u * SLICE : (u + 1) * SLICE].astype(BF)
-
-    def to_owner(i):
-        return remote(sb.at[i], rb.at[me], s1_send.at[i], s1_recv.at[me], at(i))
-
-    def from_member(i):
-        return remote(sb.at[0], rb.at[i], s1_send.at[0], s1_recv.at[i], at(i))
-
-    def to_member(i):
-        return remote(so.at[i], st.at[me], s2_send.at[i], s2_recv.at[me], at(i))
-
-    def from_owner(i):
-        return remote(so.at[0], st.at[i], s2_send.at[0], s2_recv.at[i], at(i))
-
-    def as_owner(body):
-        if N > OWNERS:
-            pl.when(me < OWNERS)(body)
-        else:
-            body()
-
-    others(OWNERS, me, lambda i: to_owner(i).start())
+            cut = slice(u * rows_z, (u + 1) * rows_z)
+            sb[p * per + u, 0] = kv_sum[cut].astype(BF)
+            sb[p * per + u, 1] = qd_sum[cut].astype(BF)
+
+    def to_owner(i, source):
+        return remote(sb.at[i], rb.at[source], s1_send.at[i], s1_recv.at[source], {"seq": i})
+
+    def to_outer(i, source):
+        return remote(tot, trecv.at[source], t_send.at[i], t_recv.at[source], {"outer": i})
+
+    def to_member(i, source):
+        return remote(so.at[i], st.at[source], s2_send.at[i], s2_recv.at[source], {"seq": i})
+
+    others(Z, z, lambda i: to_owner(i, z).start())
 
     def attend(first, second, third, keys_first, index):
         b, p = index // PAIRS, index % PAIRS
@@ -207,29 +203,45 @@
     half = PAIRS * (blocks // 2)
     lax.fori_loop(0, half, value_step, 0)
 
-    @as_owner
-    def _():
-        others(N, me, lambda i: from_member(i).wait_recv())
-        rb[me] = sb[me]
-
-        def prefix(i, carry):
-            so[i, 0] = carry.astype(BF)
-            return carry + rb[i, 0].astype(F32)
-
-        lax.fori_loop(0, N, prefix, jnp.zeros((SLICE, PAIR), F32))
-
-        def suffix(i, carry):
-            so[N - 1 - i, 1] = carry.astype(BF)
-            return carry + rb[N - 1 - i, 1].astype(F32)
-
-        lax.fori_loop(0, N, suffix, jnp.zeros((SLICE, PAIR), F32))
-        st[me] = so[me]
-        others(N, me, lambda i: to_member(i).start())
-
+    others(Z, z, lambda i: to_owner(i, i).wait_recv())
+    rb[z] = sb[z]
+    total = jnp.zeros((rows_z, PAIR), F32)
+    for i in range(Z):
+        part[i, 0] = total
+        total = total + rb[i, 0].astype(F32)
+    tot[0] = total.astype(BF)
+    total = jnp.zeros((rows_z, PAIR), F32)
+    for i in reversed(range(Z)):
+        part[i, 1] = total
+        total = total + rb[i, 1].astype(F32)
+    tot[1] = total.astype(BF)
+    others(outer_count, o, lambda i: to_outer(i, o).start())
     lax.fori_loop(half, steps, value_step, 0)
-    others(OWNERS, me, lambda i: from_owner(i).wait_recv())
-
-    per = HEAD_DIM // SLICE
+    others(outer_count, o, lambda i: to_outer(i, i).wait_recv())
+    trecv[o] = tot[...]
+    earlier = jnp.zeros((rows_z, PAIR), F32)
+    later = jnp.zeros((rows_z, PAIR), F32)
+    for i in range(outer_count):
+        earlier = earlier + trecv[i, 0].astype(F32) * jnp.where(i < o, 1.0, 0.0)
+        later = later + trecv[i, 1].astype(F32) * jnp.where(i > o, 1.0, 0.0)
+    for i in range(Z):
+        so[i, 0] = (earlier + part[i, 0]).astype(BF)
+        so[i, 1] = (later + part[i, 1]).astype(BF)
+    st[z] = so[z]
+    others(Z, z, lambda i: to_member(i, z).start())
+
+    def query_early(index, carry):
+        _, _, lanes, lo, hi, res_lo, res_hi = attend(gs, v, k, False, index)
+        gqa[lo, lanes] = res_lo
+        gqa[hi, lanes] = res_hi
+        return carry
+
+    lax.fori_loop(0, half, query_early, 0)
+    for i in range(tiles):
+        xt[:, i * TILE : (i + 1) * TILE] = inp[i * TILE : (i + 1) * TILE, :].T
+    others(Z, z, lambda i: to_member(i, i).wait_recv())
+
+    per = HEAD_DIM // rows_z
     for p in range(PAIRS):
         prev = st[p * per : (p + 1) * per, 0].astype(F32).reshape(HEAD_DIM, PAIR)
         for b in range(blocks):
@@ -335,12 +347,18 @@
         gq[hi, lanes] = (res_hi + mm(gs[hi, lanes], state, NT)).astype(BF)
         return carry
 
-    lax.fori_loop(0, half, query_step, 0)
+    def query_finish(index, carry):
+        b, p = index // PAIRS, index % PAIRS
+        lanes = pl.ds(pl.multiple_of(p * PAIR, PAIR), PAIR)
+        rows = pl.ds(pl.multiple_of(b * BLOCK, BLOCK), BLOCK)
+        gq[rows, lanes] = (gqa[rows, lanes] + mm(gs[rows, lanes], sp[b, p], NT)).astype(BF)
+        return carry
+
+    lax.fori_loop(0, half, query_finish, 0)
+    lax.fori_loop(half, steps, query_step, 0)
     stage_x(0)
-    lax.fori_loop(half, steps, query_step, 0)
     weight(1, gq)
     stage_core(1)
-    stage_z(0)
 
     def key_step(index, carry):
         b, p, lanes, lo, hi, res_lo, res_hi = attend(v, gs, q, True, index)
@@ -354,10 +372,8 @@
     send_g = remote(edge_g, edge_gr, edge_sem.at[2], edge_sem.at[3], at(ahead))
     send_g.start()
     stage_x(1)
-    stage_az(0)
+    stage_z(0)
     lax.fori_loop(half, steps, key_step, 0)
-    stage_z(1)
-    stage_ax(0)
 
     send_g.wait()
     keep_g = jnp.where(me == N - 1, 0.0, 1.0)
@@ -379,16 +395,20 @@
 
     sums = lax.fori_loop(0, tiles, pre_tile, tuple(jnp.zeros((8, D), F32) for _ in range(TAPS)))
     for j in range(TAPS):
-        cown[j : j + 1, :] = jnp.sum(sums[j], 0, keepdims=True)
-
-    def conv_copy(i, source):
-        return remote(cown, crecv.at[source], cv_send.at[i], cv_recv.at[source], at(i))
+        csend[0, j : j + 1, :] = jnp.sum(sums[j], 0, keepdims=True)
+
+    conv_core = remote(csend.at[0], crc, cv_c.at[0], cv_c.at[1], {"outer": x * 2 + 1 - core})
+
+    def conv_x(i, source):
+        return remote(csend.at[1], crx.at[source], cv_x.at[0, i], cv_x.at[1, source],
+                      {"outer": i * 2 + core})
+
+    def conv_z(i, source):
+        return remote(csend.at[2], crz.at[source], cv_z.at[0, i], cv_z.at[1, source], {"seq": i})
 
     weight(2, gp)
     stage_core(2)
-    stage_ac(0)
-    stage_az(1)
-    others(N, me, lambda i: conv_copy(i, me).start())
+    conv_core.start()
 
     def gin_tile(i, carry):
         rows = pl.ds(pl.multiple_of(i * TILE, TILE), TILE)
@@ -398,26 +418,44 @@
         gin[rows, :] = total.astype(BF)
         return carry
 
+    quarter = tiles // 4
+    lax.fori_loop(0, quarter, gin_tile, 0)
     stage_x(2)
-    lax.fori_loop(0, tiles // 2, gin_tile, 0)
+    stage_az(0)
+    stage_z(1)
+    lax.fori_loop(quarter, 2 * quarter, gin_tile, 0)
+    conv_core.wait_recv()
+    csend[1] = csend[0] + crc[...]
+    others(X, x, lambda i: conv_x(i, x).start())
+    stage_z(2)
+    stage_ax(0)
+    stage_az(1)
+    lax.fori_loop(2 * quarter, tiles, gin_tile, 0)
+    stage_az(2)
+    stage_ac(0)
     stage_ax(1)
-    stage_z(2)
-    lax.fori_loop(tiles // 2, tiles, gin_tile, 0)
+    others(X, x, lambda i: conv_x(i, i).wait_recv())
+    crx[x] = csend[1]
+    total = crx[0]
+    for i in range(1, X):
+        total = total + crx[i]
+    csend[2] = total
+    others(Z, z, lambda i: conv_z(i, z).start())
+    stage_ax(2)
     stage_ac(1)
-    stage_az(2)
-    others(N, me, lambda i: conv_copy(i, i).wait_recv())
-    crecv[me] = cown[...]
-    conv_out[...] = lax.fori_loop(
-        1, N, lambda i, total: total + crecv[i], crecv[0])
-    stage_ax(2)
     stage_ac(2)
-    others(OWNERS, me, lambda i: to_owner(i).wait_send())
-
-    @as_owner
-    def _():
-        others(N, me, lambda i: to_member(i).wait_send())
-
-    others(N, me, lambda i: conv_copy(i, me).wait_send())
+    others(Z, z, lambda i: conv_z(i, i).wait_recv())
+    crz[z] = csend[2]
+    total = crz[0]
+    for i in range(1, Z):
+        total = total + crz[i]
+    conv_out[...] = total
+    others(Z, z, lambda i: to_owner(i, z).wait_send())
+    others(outer_count, o, lambda i: to_outer(i, o).wait_send())
+    others(Z, z, lambda i: to_member(i, z).wait_send())
+    conv_core.wait_send()
+    others(X, x, lambda i: conv_x(i, x).wait_send())
+    others(Z, z, lambda i: conv_z(i, z).wait_send())
     stage_end(0)
     stage_end(1)
     stage_end(2)
@@ -434,18 +472,22 @@
     full = vm((length, D), BF)
     edge = vm((EDGE, D), BF)
     state = vm((blocks, PAIRS, HEAD_DIM, PAIR), F32)
-    member = vm((N, 2, SLICE, PAIR), BF)
-    owner = vm((OWNERS, 2, SLICE, PAIR), BF)
+    rows_z = PAIRS * HEAD_DIM // Z
+    sliced = vm((Z, 2, rows_z, PAIR), BF)
+    parts = vm((Z, 2, rows_z, PAIR), F32)
+    total = vm((2, rows_z, PAIR), BF)
+    totals = vm((outer_count, 2, rows_z, PAIR), BF)
     square = vm((blocks, PAIRS, PAIR, PAIR), BF)
     scratch = [
         vm((length + 8, D), F32), full, full, full, full, full, vm((D, length), BF),
-        vm((length, D), F32), full, vm((length + 8, D), F32), full, full,
+        vm((length, D), F32), vm((length, D), F32), full, vm((length + 8, D), F32), full, full,
         edge, edge, edge, edge,
-        state, state, owner, member, member, owner, square, square,
+        state, state, sliced, sliced, parts, total, totals, sliced, sliced, square, square,
         vm((3, 2, X, Z, r, D), BF), vm((3, X, Z, r, D), BF), vm((3, X, Z, r, D), BF),
         vm((3, X, Z, r, D), BF), vm((3, Z, r, D), BF), vm((3, Z, r, D), BF),
-        vm((TAPS, D), F32), vm((N, TAPS, D), F32),
-        dma((4,)), dma((OWNERS,)), dma((N,)), dma((N,)), dma((OWNERS,)), dma((N,)), dma((N,)),
+        vm((3, TAPS, D), F32), vm((TAPS, D), F32), vm((X, TAPS, D), F32), vm((Z, TAPS, D), F32),
+        dma((4,)), dma((Z,)), dma((Z,)), dma((outer_count,)), dma((outer_count,)), dma((Z,)), dma((Z,)),
+        dma((2,)), dma((2, X)), dma((2, Z)),
         dma((3, 2)), dma((3, X)), dma((3, X)), dma((3, Z)), dma((3, Z)),
         dma((3, Z)), dma((3, Z)), dma((3, X)), dma((3, X)), dma((3, 2)),
     ]

time: 74.2 us -> 72.1 us (0.972)
  Pallas kernels: 68.6 us -> 66.5 us
    pallas_call x1, Pallas kernels: 68.6 us -> 66.5 us  [on_device(): pl.pallas_call(functools.partial(kernel, seq_count, outer_count), out_sha...]
where the time goes in v2:
time: 72.1 us; the launch traced here: 72 us
  Pallas kernels  66.5 us (92%)
  local copies, waits for them, and re-layouts  4.82 us (7%)
    pallas_call x1, Pallas kernels, on_device(): pl.pallas_call(functools.partial(kernel, seq_count, outer_count), out_sha...  66.5 us
    slice x1, local copies, waits for them, and re-layouts, on_device(): return (grad_inputs, weights[1], weights[2], weights[0], grad_conv)  3.24 us
    unnamed x6, local copies, waits for them, and re-layouts  1.58 us

profile of v2, /device:TPU:0, one launch (start us, length us, event | category | flops | bytes accessed | tf_op | source)
XLA Modules:
  0.0 72.0 jit_solution(7078051141748314139)
XLA Ops:
  0.6 66.5 %shard_map.101 = (bf16[1024,512]{1,0:T(8,128)(2,1)}, bf16[3,2,2,4,32,512]{5,4,3,2,1,0:T(8,128)(2,1)}, f32[4,512]{1,0:T(4,128)}) custom-call(bf16[1024,512]{1,0:T(8,128)(2,1)} %inp.1, bf16[1024,512]{1,0:T(8,128)(2,1)} %go.1, bf16[512,512]{1,0:T(8,128)(2,1)} %wq.1, bf16[512,512]{1,0:T(8,128)(2,1)} %wk.1, bf16[512,512]{1,0:T(8,128)(2,1)} %wv.1, ...), custom_call_target="tpu_custom_call" | custom-call | tf_op jit(solution)/shard_map/pallas_call | solution.py:495
  67.1 0.0 copy-start
  67.1 3.2 %fusion = (f32[1,2,2,4,32,512]{5,4,3,2,1,0:T(8,128)}, f32[1,2,2,4,32,512]{5,4,3,2,1,0:T(8,128)}, f32[1,2,2,4,32,512]{5,4,3,2,1,0:T(8,128)}) fusion(bf16[3,2,2,4,32,512]{5,4,3,2,1,0:T(8,128)(2,1)} %get-tuple-element.9), kind=kLoop, calls=%fused_computation | loop fusion | bytes 6291456 | tf_op jit(solution)/shard_map/slice | solution.py:510
  70.4 0.0 copy-start.1
  70.4 0.0 copy-done
  70.4 1.0 %copy.13 = bf16[1024,512]{1,0:T(8,128)(2,1)} copy(bf16[1024,512]{1,0:T(8,128)(2,1)S(1)} %copy-done) | data formatting | bytes 2097152
  71.4 0.0 copy-done.1
  71.4 0.6 copy.14
Async XLA Ops:
  67.1 3.3 %copy-start = (bf16[1024,512]{1,0:T(8,128)(2,1)S(1)}, bf16[1024,512]{1,0:T(8,128)(2,1)}, u32[]{:S(2)}) copy-start(bf16[1024,512]{1,0:T(8,128)(2,1)} %get-tuple-element.19) | copy-start | bytes 3145732
  70.4 1.0 %copy-start.1 = (f32[4,512]{1,0:T(4,128)S(1)}, f32[4,512]{1,0:T(4,128)}, u32[]{:S(2)}) copy-start(f32[4,512]{1,0:T(4,128)} %get-tuple-element.23) | copy-start | bytes 24580
